TPU v7x, 128 devices: a whole 4x4x4 slice. The times are simulated.
128 devices in a mesh: param: 16 (over x, y_hi, core), ex: 8 (over y_lo, z).
Axes of the slice: x: 4, y: 4 (y_hi: 2, y_lo: 2; y = y_hi * 2 + y_lo), z: 4, core: 2. Of those that a mesh axis runs over, the one named last changes fastest.
Arguments:
- grads: float32 [98304, 4096], P('param', 'ex'), may hold values from -6 to 6
- projection: bfloat16 [98304, 1024], P('param'), may hold values from -6 to 6
- whitener: float32 [1024, 1024], P('param'), may hold values from -1 to 3
Outputs:
- scores: float32 [4096, 4096], P('ex', 'param')
All inputs are finite; a program needn't handle non-finite values.
Results may differ from a plain program's by a relative error of at most 0.0052.
Values may be sent and summed in bfloat16 or wider, within the bound.
No kernel may reach another device: no remote copies, remote signals or barrier semaphores. Data moves between devices by JAX's collectives and lax.ppermute only.
A program may use at most 128 MiB of HBM per device.

v0:
```python
import math
import jax
import jax.numpy as jnp
from jax import lax
from jax.sharding import PartitionSpec as P


def body(grads, projection, whitener):
    low_grads = grads.astype(jnp.bfloat16)
    partial_value = lax.dot_general(
        projection, low_grads, (((0,), (0,)), ((), ())), preferred_element_type=jnp.float32
    )
    param_count = lax.axis_size("param")
    ex_count = lax.axis_size("ex")
    norm_factor = 1.0 / math.sqrt(grads.shape[0] * param_count)
    whole_whitener = lax.all_gather(whitener, "param", axis=0, tiled=True)
    sketch_rows = partial_value.shape[0]
    local_width = grads.shape[1]
    total_width = local_width * ex_count
    tile_width = total_width // param_count
    col_start = lax.axis_index("param") * tile_width
    sketch = lax.psum(partial_value, "param") * norm_factor
    whitened = jnp.dot(whole_whitener, sketch, precision=lax.Precision.HIGHEST).astype(jnp.bfloat16)
    all_columns = lax.all_gather(whitened, "ex", axis=1, tiled=True)
    row_start = lax.axis_index("ex") * local_width
    row_block = lax.dynamic_slice_in_dim(all_columns, row_start, local_width, 1)
    col_block = lax.dynamic_slice_in_dim(all_columns, col_start, tile_width, 1)
    tile = lax.dot_general(
        row_block, col_block, (((0,), (0,)), ((), ())), preferred_element_type=jnp.float32
    )
    return tile / sketch_rows


def solution(mesh):
    return jax.shard_map(
        body,
        mesh=mesh,
        in_specs=(P("param", "ex"), P("param", None), P("param", None)),
        out_specs=P("ex", "param"),
        check_vma=False,
    )
```

profile of v0, /device:TPU:1, one launch (start us, length us, event | category | flops | bytes accessed | tf_op | source)
XLA Modules:
  0.0 344.9 jit_solution(1237545374964463168)
XLA Ops:
  6.5 0.0 all-reduce.2.cloned.1.call-start
  6.5 14.3 %fusion = f32[1024,512]{1,0:T(8,128)} fusion(bf16[6144,1024]{1,0:T(8,128)(2,1)} %param.4, f32[6144,512]{1,0:T(8,128)} %param.3), kind=kOutput, calls=%fused_computation | convolution fusion | flops 6445596672 | bytes 27262976 | tf_op jit(solution)/shard_map/dot_general | solution.py:10
  20.9 0.0 all-reduce.2.cloned.1.call-update
  20.9 0.0 all-gather.3.cloned.1.call-start
  21.0 0.7 all-gather.3.cloned.1.call-update
  21.7 0.0 all-gather.5.cloned.1.call-start
  21.7 146.6 %all-reduce.2.cloned.1.call-done = f32[1024,512]{1,0:T(8,128)} async-done(((f32[1024,512]{1,0:T(8,128)}), f32[1024,512]{1,0:T(8,128)}) %all-reduce.2.cloned.1.call-update) | async-done | bytes 2097168 | tf_op jit(solution)/shard_map/psum | solution.py:22
  168.3 60.1 %all-gather.3.cloned.1.call-done = f32[1024,1024]{1,0:T(8,128)} async-done(((f32[64,1024]{1,0:T(8,128)}), f32[1024,1024]{1,0:T(8,128)}) %all-gather.3.cloned.1.call-update) | async-done | bytes 4194320 | tf_op jit(solution)/shard_map/all_gather | solution.py:16
  228.4 16.6 %fusion.7 = bf16[1024,512]{0,1:T(8,128)(2,1)} fusion(f32[1024,1024]{1,0:T(8,128)} %all-gather.3.cloned.1.call-done, f32[1024,512]{1,0:T(8,128)} %all-reduce.2.cloned.1.call-done), kind=kOutput, calls=%fused_computation.5 | convolution fusion | flops 6443499520 | bytes 7340032 | tf_op jit(solution)/shard_map/dot_general | solution.py:23
  245.0 0.0 all-gather.5.cloned.1.call-update
  245.0 90.7 %all-gather.5.cloned.1.call-done = bf16[1024,4096]{0,1:T(8,128)(2,1)} async-done(((bf16[1024,512]{0,1:T(8,128)(2,1)}), bf16[1024,4096]{0,1:T(8,128)(2,1)}) %all-gather.5.cloned.1.call-update) | async-done | bytes 8388624 | tf_op jit(solution)/shard_map/all_gather | solution.py:24
  335.7 2.6 convolution_multiply_fusion
Async XLA Ops:
  6.5 161.7 %all-reduce.2.cloned.1.call-start = ((), (), s32[]{:S(2)}) async-start(), calls=%async_computation | async-start | bytes 4194304 | tf_op jit(solution)/shard_map/psum | solution.py:22
  20.9 207.5 %all-gather.3.cloned.1.call-start = ((), (), s32[]{:S(2)}) async-start(), calls=%async_computation.1 | async-start | bytes 4456448 | tf_op jit(solution)/shard_map/all_gather | solution.py:16
  21.7 314.1 %all-gather.5.cloned.1.call-start = ((), (), s32[]{:S(2)}) async-start(), calls=%async_computation.2 | async-start | bytes 9437184 | tf_op jit(solution)/shard_map/all_gather | solution.py:24
Sparse Core Ops, SparseCore 0:
  21.0 147.1 all-reduce.1
  170.7 57.6 all-gather.2
  245.1 90.5 all-gather.4
where the time goes:
time: 345 us
  waiting for transfers between devices  298 us (86%)
  matrix products  33.6 us (10%)
  between operations  13.1 us (4%)
    psum x1, waiting for transfers between devices, body(): sketch = lax.psum(partial_value, 'param') * norm_factor  147 us
    all_gather x1, waiting for transfers between devices, body(): all_columns = lax.all_gather(whitened, 'ex', axis=1, tiled=True)  90.7 us
    all_gather x1, waiting for transfers between devices, body(): whole_whitener = lax.all_gather(whitener, 'param', axis=0, tiled=True)  60.1 us
    dot_general x1, matrix products, body(): jnp.dot(whole_whitener, sketch, precision=lax.Precision.HIGHEST)  16.6 us
    dot_general x1, matrix products, body(): lax.dot_general(projection, low_grads, (((0,), (0,)), ((), ())), preferre...  14.3 us
  transfers between devices with their start and end apart: 3, of which 3 were waited for; matrix products, arithmetic and copies ran while one was open for 0% of the time, Pallas kernels for 0%

commit v1 on v0

--- a/solution.py
+++ b/solution.py
@@ -13,7 +13,9 @@
     param_count = lax.axis_size("param")
     ex_count = lax.axis_size("ex")
     norm_factor = 1.0 / math.sqrt(grads.shape[0] * param_count)
-    whole_whitener = lax.all_gather(whitener, "param", axis=0, tiled=True)
+    whole_whitener = jnp.concatenate(
+        lax.all_to_all(jnp.stack([whitener] * lax.axis_size("param")), "param", 0, 0), axis=0
+    )
     sketch_rows = partial_value.shape[0]
     local_width = grads.shape[1]
     total_width = local_width * ex_count

time: 345 us -> 318 us (0.922)
  waiting for transfers between devices: 298 us -> 259 us
  starting transfers between devices: 0.08 us -> 8.52 us
  local copies, waits for them, and re-layouts: 0 us -> 3.45 us
    all_gather x1 -> x0, waiting for transfers between devices: 60.1 us -> none  [body(): whole_whitener = lax.all_gather(whitener, 'param', axis=0, tiled=True)]
    psum x1, waiting for transfers between devices: 147 us -> 166 us  [body(): sketch = lax.psum(partial_value, 'param') * norm_factor]
    all_to_all x0 -> x1, starting transfers between devices: none -> 8.45 us  [body(): lax.all_to_all(jnp.stack([whitener] * lax.axis_size('param')), 'param', 0...]
  transfers between devices with their start and end apart: 3 -> 3, of which waited for: 3 -> 2; matrix products, arithmetic and copies ran while one was open for 0% -> 4% of each run, Pallas kernels for 0% -> 0%
where the time goes in v1:
time: 318 us
  waiting for transfers between devices  259 us (81%)
  matrix products  33.5 us (11%)
  between operations  13.4 us (4%)
  starting transfers between devices  8.52 us (3%)
  local copies, waits for them, and re-layouts  3.45 us (1%)
    psum x1, waiting for transfers between devices, body(): sketch = lax.psum(partial_value, 'param') * norm_factor  166 us
    all_gather x1, waiting for transfers between devices, body(): all_columns = lax.all_gather(whitened, 'ex', axis=1, tiled=True)  93.6 us
    dot_general x1, matrix products, body(): jnp.dot(whole_whitener, sketch, precision=lax.Precision.HIGHEST)  16.6 us
    dot_general x1, matrix products, body(): lax.dot_general(projection, low_grads, (((0,), (0,)), ((), ())), preferre...  14.3 us
    all_to_all x1, starting transfers between devices, body(): lax.all_to_all(jnp.stack([whitener] * lax.axis_size('param')), 'param', 0...  8.45 us
  transfers between devices with their start and end apart: 3, of which 2 were waited for; matrix products, arithmetic and copies ran while one was open for 4% of the time, Pallas kernels for 0%

profile of v1, /device:TPU:1, one launch (start us, length us, event | category | flops | bytes accessed | tf_op | source)
XLA Modules:
  0.0 318.1 jit_solution(13056351178425769629)
XLA Ops:
  6.5 3.4 %stack.2 = f32[16,64,1024]{2,1,0:T(8,128)} broadcast(f32[64,1024]{1,0:T(8,128)} %param.5), dimensions={1,2} | broadcast | bytes 4456448 | tf_op jit(solution)/shard_map/stack | solution.py:17
  10.0 8.4 %all-to-all-start = ((f32[16,64,1024]{2,1,0:T(8,128)}), f32[16,64,1024]{2,1,0:T(8,128)}, u32[]{:S(2)}, u32[]{:S(2)}) async-start(f32[16,64,1024]{2,1,0:T(8,128)} %stack.2), calls=%async_computation | async-start | bytes 8388608 | tf_op jit(solution)/shard_map/all_to_all | solution.py:17
  18.4 0.0 all-reduce.2.cloned.1.call-start
  18.5 14.3 %fusion = f32[1024,512]{1,0:T(8,128)} fusion(bf16[6144,1024]{1,0:T(8,128)(2,1)} %param.4, f32[6144,512]{1,0:T(8,128)} %param.3), kind=kOutput, calls=%fused_computation | convolution fusion | flops 6445596672 | bytes 27262976 | tf_op jit(solution)/shard_map/dot_general | solution.py:10
  32.8 0.0 all-reduce.2.cloned.1.call-update
  32.8 0.0 all-gather.2.cloned.1.call-start
  32.8 165.6 %all-reduce.2.cloned.1.call-done = f32[1024,512]{1,0:T(8,128)} async-done(((f32[1024,512]{1,0:T(8,128)}), f32[1024,512]{1,0:T(8,128)}) %all-reduce.2.cloned.1.call-update) | async-done | bytes 2097168 | tf_op jit(solution)/shard_map/psum | solution.py:24
  198.4 0.0 all-to-all-done
  198.4 16.6 %fusion.7 = bf16[1024,512]{0,1:T(8,128)(2,1)} fusion(f32[1024,1024]{1,0:T(8,128)} %bitcast, f32[1024,512]{1,0:T(8,128)} %all-reduce.2.cloned.1.call-done), kind=kOutput, calls=%fused_computation.5 | convolution fusion | flops 6443499520 | bytes 7340032 | tf_op jit(solution)/shard_map/dot_general | solution.py:25
  215.0 0.0 all-gather.2.cloned.1.call-update
  215.0 93.6 %all-gather.2.cloned.1.call-done = bf16[1024,4096]{0,1:T(8,128)(2,1)} async-done(((bf16[1024,512]{0,1:T(8,128)(2,1)}), bf16[1024,4096]{0,1:T(8,128)(2,1)}) %all-gather.2.cloned.1.call-update) | async-done | bytes 8388624 | tf_op jit(solution)/shard_map/all_gather | solution.py:26
  308.6 2.6 convolution_multiply_fusion
Async XLA Ops:
  10.0 188.5 %all-to-all-start = ((f32[16,64,1024]{2,1,0:T(8,128)}), f32[16,64,1024]{2,1,0:T(8,128)}, u32[]{:S(2)}, u32[]{:S(2)}) async-start(f32[16,64,1024]{2,1,0:T(8,128)} %stack.2), calls=%async_computation | async-start | bytes 8388608 | tf_op jit(solution)/shard_map/all_to_all | solution.py:17
  18.4 180.0 %all-reduce.2.cloned.1.call-start = ((), (), s32[]{:S(2)}) async-start(), calls=%async_computation.1 | async-start | bytes 4194304 | tf_op jit(solution)/shard_map/psum | solution.py:24
  32.8 275.8 %all-gather.2.cloned.1.call-start = ((), (), s32[]{:S(2)}) async-start(), calls=%async_computation.2 | async-start | bytes 9437184 | tf_op jit(solution)/shard_map/all_gather | solution.py:26
Sparse Core Ops, SparseCore 0:
  32.9 165.4 all-reduce.1
  215.2 93.4 all-gather.1

commit v2 on v0

--- a/solution.py
+++ b/solution.py
@@ -19,7 +19,7 @@
     total_width = local_width * ex_count
     tile_width = total_width // param_count
     col_start = lax.axis_index("param") * tile_width
-    sketch = lax.psum(partial_value, "param") * norm_factor
+    sketch = jnp.sum(lax.all_gather(partial_value, "param"), axis=0) * norm_factor
     whitened = jnp.dot(whole_whitener, sketch, precision=lax.Precision.HIGHEST).astype(jnp.bfloat16)
     all_columns = lax.all_gather(whitened, "ex", axis=1, tiled=True)
     row_start = lax.axis_index("ex") * local_width

time: 345 us -> 384 us (1.11)
  waiting for transfers between devices: 298 us -> 325 us
  other arithmetic: 0 us -> 12.8 us
    all_gather x0 -> x1, waiting for transfers between devices: none -> 191 us  [body(): lax.all_gather(partial_value, 'param')]
    psum x1 -> x0, waiting for transfers between devices: 147 us -> none  [body(): sketch = lax.psum(partial_value, 'param') * norm_factor]
    all_gather x1, waiting for transfers between devices: 60.1 us -> 43.1 us  [body(): whole_whitener = lax.all_gather(whitener, 'param', axis=0, tiled=True)]
    reduce_sum x0 -> x1, other arithmetic: none -> 12.8 us  [body(): jnp.sum(lax.all_gather(partial_value, 'param'), axis=0) * norm_factor]
  transfers between devices with their start and end apart: 3 -> 3, of which waited for: 3 -> 3; matrix products, arithmetic and copies ran while one was open for 0% -> 3% of each run, Pallas kernels for 0% -> 0%
where the time goes in v2:
time: 384 us
  waiting for transfers between devices  325 us (85%)
  matrix products  33 us (9%)
  between operations  13.1 us (3%)
  other arithmetic  12.8 us (3%)
    all_gather x1, waiting for transfers between devices, body(): lax.all_gather(partial_value, 'param')  191 us
    all_gather x1, waiting for transfers between devices, body(): all_columns = lax.all_gather(whitened, 'ex', axis=1, tiled=True)  90.7 us
    all_gather x1, waiting for transfers between devices, body(): whole_whitener = lax.all_gather(whitener, 'param', axis=0, tiled=True)  43.1 us
    dot_general x1, matrix products, body(): jnp.dot(whole_whitener, sketch, precision=lax.Precision.HIGHEST)  16 us
    dot_general x1, matrix products, body(): lax.dot_general(projection, low_grads, (((0,), (0,)), ((), ())), preferre...  14.4 us
    reduce_sum x1, other arithmetic, body(): jnp.sum(lax.all_gather(partial_value, 'param'), axis=0) * norm_factor  12.8 us
  transfers between devices with their start and end apart: 3, of which 3 were waited for; matrix products, arithmetic and copies ran while one was open for 3% of the time, Pallas kernels for 0%

profile of v2, /device:TPU:1, one launch (start us, length us, event | category | flops | bytes accessed | tf_op | source)
XLA Modules:
  0.0 384.2 jit_solution(12166970372623265708)
XLA Ops:
  6.5 0.0 all-gather.9.cloned.1.call-start
  6.5 14.4 %fusion = f32[1024,512]{1,0:T(8,128)} fusion(bf16[6144,1024]{1,0:T(8,128)(2,1)} %param.4, f32[6144,512]{1,0:T(8,128)} %param.3), kind=kOutput, calls=%fused_computation | convolution fusion | flops 6445596672 | bytes 27262976 | tf_op jit(solution)/shard_map/dot_general | solution.py:10
  21.0 0.0 all-gather.9.cloned.1.call-update
  21.0 0.0 all-gather.5.cloned.1.call-start
  21.0 0.7 all-gather.5.cloned.1.call-update
  21.7 0.0 all-gather.7.cloned.1.call-start
  21.8 190.6 %all-gather.9.cloned.1.call-done = f32[16384,512]{1,0:T(8,128)} async-done(((f32[1024,512]{1,0:T(8,128)}), f32[16384,512]{1,0:T(8,128)}) %all-gather.9.cloned.1.call-update) | async-done | bytes 33554448 | tf_op jit(solution)/shard_map/all_gather | solution.py:22
  212.4 12.8 %reduce_sum.9 = f32[1024,512]{1,0:T(8,128)S(1)} reduce(f32[16,1024,512]{2,1,0:T(8,128)} %bitcast.5, f32[]{:T(128)} %constant.4.clone.1), dimensions={0}, to_apply=%region_0.0 | reduce | flops 7864320 | bytes 35651588 | tf_op jit(solution)/shard_map/reduce_sum | solution.py:22
  225.2 43.1 %all-gather.5.cloned.1.call-done = f32[1024,1024]{1,0:T(8,128)} async-done(((f32[64,1024]{1,0:T(8,128)}), f32[1024,1024]{1,0:T(8,128)}) %all-gather.5.cloned.1.call-update) | async-done | bytes 4194320 | tf_op jit(solution)/shard_map/all_gather | solution.py:16
  268.4 16.0 %fusion.7 = bf16[1024,512]{0,1:T(8,128)(2,1)} fusion(f32[1024,1024]{1,0:T(8,128)} %all-gather.5.cloned.1.call-done, f32[1024,512]{1,0:T(8,128)S(1)} %reduce_sum.9), kind=kOutput, calls=%fused_computation.5 | convolution fusion | flops 6443499520 | bytes 7340032 | tf_op jit(solution)/shard_map/dot_general | solution.py:23
  284.3 0.0 all-gather.7.cloned.1.call-update
  284.4 90.7 %all-gather.7.cloned.1.call-done = bf16[1024,4096]{0,1:T(8,128)(2,1)} async-done(((bf16[1024,512]{0,1:T(8,128)(2,1)}), bf16[1024,4096]{0,1:T(8,128)(2,1)}) %all-gather.7.cloned.1.call-update) | async-done | bytes 8388624 | tf_op jit(solution)/shard_map/all_gather | solution.py:24
  375.1 2.6 convolution_multiply_fusion
Async XLA Ops:
  6.5 205.9 %all-gather.9.cloned.1.call-start = ((), (), s32[]{:S(2)}) async-start(), calls=%async_computation.2 | async-start | bytes 35651584 | tf_op jit(solution)/shard_map/all_gather | solution.py:22
  21.0 247.4 %all-gather.5.cloned.1.call-start = ((), (), s32[]{:S(2)}) async-start(), calls=%async_computation | async-start | bytes 4456448 | tf_op jit(solution)/shard_map/all_gather | solution.py:16
  21.7 353.3 %all-gather.7.cloned.1.call-start = ((), (), s32[]{:S(2)}) async-start(), calls=%async_computation.1 | async-start | bytes 9437184 | tf_op jit(solution)/shard_map/all_gather | solution.py:24
Sparse Core Ops, SparseCore 0:
  21.1 191.2 all-gather.8
  214.8 53.5 all-gather.4
  284.5 90.5 all-gather.6
